TPU v7x, 32 devices: a whole 2x2x4 slice. The times are simulated.
32 devices in a mesh: parts: 2 (over y), latent: 16 (over z, x, core).
Axes of the slice: x: 2, y: 2, z: 4, core: 2. Of those that a mesh axis runs over, the one named last changes fastest.
Arguments:
- residual: bfloat16 [512, 4608], P(('parts', 'latent')), parts along dimension 0, may hold values from -6 to 6
- enc_weight: bfloat16 [4608, 8192], P(None, 'latent'), may hold values from -0.09375 to 0.09375
- enc_bias: float32 [8192], P('latent'), may hold values from -3 to 3
- threshold: float32 [8192], P('latent'), may hold values from 0.3 to 2
- dec_weight: bfloat16 [8192, 4608], P('latent'), may hold values from -0.1875 to 0.1875
- dec_bias: float32 [4608], replicated, may hold values from -3 to 3
- pre_gain: float32 [4608], replicated, may hold values from 0.1 to 1.9
- gate_weight: bfloat16 [4608, 2304], P(None, 'latent'), may hold values from -0.09375 to 0.09375
- up_weight: bfloat16 [4608, 2304], P(None, 'latent'), may hold values from -0.09375 to 0.09375
- down_weight: bfloat16 [2304, 4608], P('latent'), may hold values from -0.125 to 0.125
- post_gain: float32 [4608], replicated, may hold values from 0.1 to 1.9
Outputs:
- spliced_out: bfloat16 [512, 4608], P(('parts', 'latent')), parts along dimension 0
There are 2 independent parts, one for each index of `parts`. A program takes and returns all parts, laid end to end along the dimension named above; an argument that names none is the same for every part. Nothing has to cross between parts.
All inputs are finite; a program needn't handle non-finite values.
Results may differ from a plain program's by a relative error of at most 0.0057.
Values may be sent and summed in bfloat16 or wider, within the bound.
No kernel may reach another device: no remote copies, remote signals or barrier semaphores. Data moves between devices by JAX's collectives and lax.ppermute only.
A program may use at most 128 MiB of HBM per device.

v0:
```python
import jax
import jax.numpy as jnp
from jax import lax
from jax.sharding import PartitionSpec as P

sharpness = 10.0
epsilon = 1e-06


def rms_scale(values, gain):
    return values * lax.rsqrt(jnp.mean(values * values, axis=-1, keepdims=True) + epsilon) * gain


def per_device(
    residual,
    enc_weight,
    enc_bias,
    threshold,
    dec_weight,
    dec_bias,
    pre_gain,
    gate_weight,
    up_weight,
    down_weight,
    post_gain,
):

    def encode(block_rows):
        preact = jnp.dot(block_rows, enc_weight, preferred_element_type=jnp.float32) + enc_bias
        return (preact * jax.nn.sigmoid(sharpness * (preact - threshold))).astype(jnp.bfloat16)

    def feed_hidden(block_rows):
        gate_proj = jnp.dot(block_rows, gate_weight, preferred_element_type=jnp.float32)
        up_proj = jnp.dot(block_rows, up_weight, preferred_element_type=jnp.float32)
        return (jax.nn.gelu(gate_proj, approximate=True) * up_proj).astype(jnp.bfloat16)

    def splice(local_rows):
        latent_acts = encode(lax.all_gather(local_rows, "latent", axis=0, tiled=True))
        chosen = latent_acts
        rebuilt = (
            lax.psum_scatter(
                jnp.dot(chosen, dec_weight, preferred_element_type=jnp.float32),
                "latent",
                scatter_dimension=0,
                tiled=True,
            )
            + dec_bias
        )
        normed = rms_scale(rebuilt, pre_gain).astype(jnp.bfloat16)
        hidden = feed_hidden(lax.all_gather(normed, "latent", axis=0, tiled=True))
        chosen = hidden
        ffn_sum = lax.psum_scatter(
            jnp.dot(chosen, down_weight, preferred_element_type=jnp.float32),
            "latent",
            scatter_dimension=0,
            tiled=True,
        )
        return (rebuilt + rms_scale(ffn_sum, post_gain)).astype(jnp.bfloat16)

    portions = [residual]
    results = [splice(portion) for portion in portions]
    return results[0]


def solution(mesh):
    return jax.shard_map(
        per_device,
        mesh=mesh,
        in_specs=(
            P(("parts", "latent"), None),
            P(None, "latent"),
            P("latent"),
            P("latent"),
            P("latent", None),
            P(),
            P(),
            P(None, "latent"),
            P(None, "latent"),
            P("latent", None),
            P(),
        ),
        out_specs=P(("parts", "latent"), None),
        check_vma=False,
    )
```

profile of v0, /device:TPU:0, one launch (start us, length us, event | category | flops | bytes accessed | tf_op | source)
XLA Modules:
  0.0 276.6 jit_solution(1392521232975287917)
XLA Ops:
  6.5 0.0 copy-start
  6.5 0.0 all-gather.3.cloned.1.call-start
  6.5 0.7 all-gather.3.cloned.1.call-update
  7.3 0.0 reduce-scatter.3.cloned.1.call-start
  7.3 47.4 %all-gather.3.cloned.1.call-done = bf16[256,4608]{1,0:T(8,128)(2,1)} async-done(((bf16[16,4608]{1,0:T(8,128)(2,1)}), bf16[256,4608]{1,0:T(8,128)(2,1)}) %all-gather.3.cloned.1.call-update) | async-done | bytes 2359312 | tf_op jit(solution)/shard_map/all_gather | solution.py:38
  54.7 9.4 %fusion.2 = f32[256,4608]{1,0:T(8,128)} fusion(bf16[512,4608]{1,0:T(8,128)(2,1)} %param.15, bf16[256,4608]{1,0:T(8,128)(2,1)} %all-gather.3.cloned.1.call-done, bf16[4608,512]{1,0:T(8,128)(2,1)} %param.12, f32[512]{0:T(512)} %param.14, f32[512]{0:T(512)} %param.13), kind=kOutput, calls=%fused_computation.5 | convolution fusion | flops 2416967680 | bytes 16519168 | tf_op jit(solution)/shard_map/dot_general | solution.py:42
  64.1 0.0 copy-start.3
  64.1 0.0 copy-start.4
  64.1 0.0 reduce-scatter.3.cloned.1.call-update
  64.1 0.0 copy-start.2
  64.1 0.0 all-gather.5.cloned.1.call-start
  64.1 74.4 %reduce-scatter.3.cloned.1.call-done = f32[16,4608]{1,0:T(8,128)} async-done(((f32[256,4608]{1,0:T(8,128)}), f32[16,4608]{1,0:T(8,128)}) %reduce-scatter.3.cloned.1.call-update) | async-done | bytes 294928 | tf_op jit(solution)/shard_map/reduce_scatter | solution.py:41
  138.6 0.0 copy-done.3
  138.6 1.1 multiply_reduce_fusion.1
  139.7 0.0 copy-done.4
  139.7 1.7 multiply_convert_fusion.1
  141.4 0.0 all-gather.5.cloned.1.call-update
  141.4 0.0 reduce-scatter.5.cloned.1.call-start
  141.5 41.6 %all-gather.5.cloned.1.call-done = bf16[256,4608]{1,0:T(8,128)(2,1)} async-done(((bf16[16,4608]{1,0:T(8,128)(2,1)}), bf16[256,4608]{1,0:T(8,128)(2,1)}) %all-gather.5.cloned.1.call-update) | async-done | bytes 2359312 | tf_op jit(solution)/shard_map/all_gather | solution.py:50
  183.1 2.9 %fusion.25 = f32[256,144]{0,1:T(8,128)S(1)} fusion(bf16[256,4608]{1,0:T(8,128)(2,1)} %all-gather.5.cloned.1.call-done, bf16[4608,144]{0,1:T(8,128)(2,1)} %param.18), kind=kOutput, calls=%fused_computation.34 | convolution fusion | flops 339738624 | bytes 3833856 | tf_op jit(solution)/shard_map/dot_general | solution.py:33
  186.0 0.0 copy-done
  186.0 0.0 copy-done.2
  186.0 6.6 %fusion.1 = f32[256,4608]{1,0:T(8,128)} fusion(bf16[144,4608]{1,0:T(8,128)(2,1)S(1)} %copy-done, bf16[256,4608]{1,0:T(8,128)(2,1)} %all-gather.5.cloned.1.call-done, bf16[4608,144]{0,1:T(8,128)(2,1)S(1)} %copy-done.2, f32[256,144]{0,1:T(8,128)S(1)} %fusion.25), kind=kOutput, calls=%fused_computation.3 | convolution fusion | flops 679845888 | bytes 9879552 | tf_op jit(solution)/shard_map/dot_general | solution.py:53
  192.7 0.0 copy-start.1
  192.7 0.0 copy-start.5
  192.7 0.0 reduce-scatter.5.cloned.1.call-update
  192.7 74.5 %reduce-scatter.5.cloned.1.call-done = f32[16,4608]{1,0:T(8,128)} async-done(((f32[256,4608]{1,0:T(8,128)}), f32[16,4608]{1,0:T(8,128)}) %reduce-scatter.5.cloned.1.call-update) | async-done | bytes 294928 | tf_op jit(solution)/shard_map/reduce_scatter | solution.py:52
  267.2 1.1 multiply_reduce_fusion
  268.3 0.0 copy-done.1
  268.3 0.0 copy-done.5
  268.3 1.7 add_convert_fusion
  (2 shorter events, 0.0 us)
Async XLA Ops:
  6.5 179.5 %copy-start = (bf16[144,4608]{1,0:T(8,128)(2,1)S(1)}, bf16[144,4608]{1,0:T(8,128)(2,1)}, u32[]{:S(2)}) copy-start(bf16[144,4608]{1,0:T(8,128)(2,1)} %param.20) | copy-start | bytes 3981316
  6.5 48.1 %all-gather.3.cloned.1.call-start = ((), (), s32[]{:S(2)}) async-start(), calls=%async_computation.2 | async-start | bytes 2506752 | tf_op jit(solution)/shard_map/all_gather | solution.py:38
  7.3 131.3 %reduce-scatter.3.cloned.1.call-start = ((), (), s32[]{:S(2)}) async-start(), calls=%async_computation.3 | async-start | bytes 5013504 | tf_op jit(solution)/shard_map/reduce_scatter | solution.py:41
  64.1 74.5 %copy-start.3 = (f32[4608]{0:T(1024)S(1)}, f32[4608]{0:T(1024)}, u32[]{:S(2)}) copy-start(f32[4608]{0:T(1024)} %param.16) | copy-start | bytes 55300
  64.1 75.6 %copy-start.4 = (f32[4608]{0:T(1024)S(1)}, f32[4608]{0:T(1024)}, u32[]{:S(2)}) copy-start(f32[4608]{0:T(1024)} %param.17) | copy-start | bytes 55300
  64.1 122.0 %copy-start.2 = (bf16[4608,144]{0,1:T(8,128)(2,1)S(1)}, bf16[4608,144]{0,1:T(8,128)(2,1)}, u32[]{:S(2)}) copy-start(bf16[4608,144]{0,1:T(8,128)(2,1)} %param.19) | copy-start | bytes 3981316
  64.1 119.0 %all-gather.5.cloned.1.call-start = ((), (), s32[]{:S(2)}) async-start(), calls=%async_computation.4 | async-start | bytes 2506752 | tf_op jit(solution)/shard_map/all_gather | solution.py:50
  141.4 125.7 %reduce-scatter.5.cloned.1.call-start = ((), (), s32[]{:S(2)}) async-start(), calls=%async_computation.5 | async-start | bytes 5013504 | tf_op jit(solution)/shard_map/reduce_scatter | solution.py:52
  192.7 75.6 %copy-start.1 = (f32[16,4608]{1,0:T(8,128)S(1)}, f32[16,4608]{1,0:T(8,128)}, u32[]{:S(2)}) copy-start(f32[16,4608]{1,0:T(8,128)} %reduce-scatter.3.cloned.1.call-done) | copy-start | bytes 884740
  192.7 75.6 %copy-start.5 = (f32[4608]{0:T(1024)S(1)}, f32[4608]{0:T(1024)}, u32[]{:S(2)}) copy-start(f32[4608]{0:T(1024)} %param.21) | copy-start | bytes 55300
Sparse Core Ops, SparseCore 0:
  9.6 45.0 all-gather.2
  64.2 74.3 reduce-scatter.2
  141.5 41.4 all-gather.4
  192.8 74.3 reduce-scatter.4
where the time goes:
time: 277 us
  waiting for transfers between devices  239 us (86%)
  matrix products  18.9 us (7%)
  between operations  13.2 us (5%)
  other arithmetic  5.68 us (2%)
    reduce_scatter x1, waiting for transfers between devices, splice(): lax.psum_scatter(jnp.dot(chosen, down_weight, preferred_element_type=jnp....  74.5 us
    reduce_scatter x1, waiting for transfers between devices, splice(): lax.psum_scatter(jnp.dot(chosen, dec_weight, preferred_element_type=jnp.f...  74.4 us
    all_gather x1, waiting for transfers between devices, splice(): lax.all_gather(local_rows, 'latent', axis=0, tiled=True)  47.4 us
    all_gather x1, waiting for transfers between devices, splice(): hidden = feed_hidden(lax.all_gather(normed, 'latent', axis=0, tiled=True))  41.6 us
    dot_general x1, matrix products, splice(): jnp.dot(chosen, dec_weight, preferred_element_type=jnp.float32)  9.37 us
    dot_general x1, matrix products, splice(): jnp.dot(chosen, down_weight, preferred_element_type=jnp.float32)  6.61 us
  transfers between devices with their start and end apart: 4, of which 4 were waited for; matrix products, arithmetic and copies ran while one was open for 0% of the time, Pallas kernels for 0%

commit v1 on v0

--- a/solution.py
+++ b/solution.py
@@ -5,6 +5,18 @@
 
 sharpness = 10.0
 epsilon = 1e-06
+
+
+def doubled_up(shard, axis, dim):
+    ways, here = (lax.axis_size(axis), lax.axis_index(axis))
+    grown, reach = (shard, 1)
+    while reach < ways:
+        theirs = lax.ppermute(grown, axis, [(d, d ^ reach) for d in range(ways)])
+        mine_first = jnp.concatenate([grown, theirs], axis=dim)
+        theirs_first = jnp.concatenate([theirs, grown], axis=dim)
+        grown = jnp.where(here & reach == 0, mine_first, theirs_first)
+        reach = 2 * reach
+    return grown
 
 
 def rms_scale(values, gain):
@@ -35,7 +47,7 @@
         return (jax.nn.gelu(gate_proj, approximate=True) * up_proj).astype(jnp.bfloat16)
 
     def splice(local_rows):
-        latent_acts = encode(lax.all_gather(local_rows, "latent", axis=0, tiled=True))
+        latent_acts = encode(doubled_up(local_rows, "latent", 0))
         chosen = latent_acts
         rebuilt = (
             lax.psum_scatter(

time: 277 us -> 313 us (1.13)
  waiting for transfers between devices: 239 us -> 265 us
  starting transfers between devices: 0.13 us -> 8.06 us
    ppermute x0 -> x4, waiting for transfers between devices: none -> 71.9 us  [doubled_up(): theirs = lax.ppermute(grown, axis, [(d, d ^ reach) for d in range(ways)])]
    all_gather x1 -> x0, waiting for transfers between devices: 47.4 us -> none  [splice(): lax.all_gather(local_rows, 'latent', axis=0, tiled=True)]
    ppermute x0 -> x4, starting transfers between devices: none -> 7.98 us  [doubled_up(): theirs = lax.ppermute(grown, axis, [(d, d ^ reach) for d in range(ways)])]
  transfers between devices with their start and end apart: 4 -> 7, of which waited for: 4 -> 7; matrix products, arithmetic and copies ran while one was open for 0% -> 0% of each run, Pallas kernels for 0% -> 0%
where the time goes in v1:
time: 313 us
  waiting for transfers between devices  265 us (85%)
  matrix products  18.8 us (6%)
  between operations  13.2 us (4%)
  other arithmetic  8.3 us (3%)
  starting transfers between devices  8.06 us (3%)
    reduce_scatter x1, waiting for transfers between devices, splice(): lax.psum_scatter(jnp.dot(chosen, dec_weight, preferred_element_type=jnp.f...  76.5 us
    reduce_scatter x1, waiting for transfers between devices, splice(): lax.psum_scatter(jnp.dot(chosen, down_weight, preferred_element_type=jnp....  74.4 us
    ppermute x4, waiting for transfers between devices, doubled_up(): theirs = lax.ppermute(grown, axis, [(d, d ^ reach) for d in range(ways)])  71.9 us
    all_gather x1, waiting for transfers between devices, splice(): hidden = feed_hidden(lax.all_gather(normed, 'latent', axis=0, tiled=True))  41.6 us
    dot_general x1, matrix products, splice(): jnp.dot(chosen, dec_weight, preferred_element_type=jnp.float32)  9.3 us
    ppermute x4, starting transfers between devices, doubled_up(): theirs = lax.ppermute(grown, axis, [(d, d ^ reach) for d in range(ways)])  7.98 us
    dot_general x1, matrix products, splice(): jnp.dot(chosen, down_weight, preferred_element_type=jnp.float32)  6.62 us
  transfers between devices with their start and end apart: 7, of which 7 were waited for; matrix products, arithmetic and copies ran while one was open for 0% of the time, Pallas kernels for 0%

profile of v1, /device:TPU:0, one launch (start us, length us, event | category | flops | bytes accessed | tf_op | source)
XLA Modules:
  0.0 312.9 jit_solution(793490148362850727)
XLA Ops:
  6.5 0.0 copy-start
  6.5 0.0 copy-start.6
  6.5 0.0 copy-start.7
  6.5 0.0 reduce-scatter.3.cloned.1.call-start
  6.5 0.6 collective-permute-start
  7.1 1.2 collective-permute-done
  8.3 1.0 maximum_select_fusion.10
  9.4 2.9 collective-permute-start.1
  12.3 7.3 %collective-permute-done.1 = bf16[32,4608]{1,0:T(8,128)(2,1)S(1)} collective-permute-done((bf16[32,4608]{1,0:T(8,128)(2,1)S(1)}, bf16[32,4608]{1,0:T(8,128)(2,1)S(1)}, u32[]{:S(2)}, u32[]{:S(2)}) %collective-permute-start.1) | collective-permute-done | bytes 294944 | tf_op jit(solution)/shard_map/ppermute | solution.py:14
  19.6 0.1 maximum_select_fusion.5
  19.7 1.9 collective-permute-start.2
  21.6 13.1 %collective-permute-done.2 = bf16[64,4608]{1,0:T(8,128)(2,1)} collective-permute-done((bf16[64,4608]{1,0:T(8,128)(2,1)S(1)}, bf16[64,4608]{1,0:T(8,128)(2,1)}, u32[]{:S(2)}, u32[]{:S(2)}) %collective-permute-start.2) | collective-permute-done | bytes 589856 | tf_op jit(solution)/shard_map/ppermute | solution.py:14
  34.7 1.5 maximum_select_fusion.4
  36.1 2.6 collective-permute-start.3
  38.8 50.3 %collective-permute-done.3 = bf16[128,4608]{1,0:T(8,128)(2,1)} collective-permute-done((bf16[128,4608]{1,0:T(8,128)(2,1)S(1)}, bf16[128,4608]{1,0:T(8,128)(2,1)}, u32[]{:S(2)}, u32[]{:S(2)}) %collective-permute-start.3) | collective-permute-done | bytes 1179680 | tf_op jit(solution)/shard_map/ppermute | solution.py:14
  89.1 0.0 copy-done.6
  89.1 0.0 copy-done.7
  89.1 9.3 %fusion.10 = f32[256,4608]{1,0:T(8,128)} fusion(bf16[512,4608]{1,0:T(8,128)(2,1)} %param.15, bf16[4608,512]{1,0:T(8,128)(2,1)} %param.12, bf16[128,4608]{1,0:T(8,128)(2,1)} %collective-permute-done.3, bf16[128,4608]{1,0:T(8,128)(2,1)S(1)} %maximum_select_fusion.4, pred[]{:T(512)S(6)} %eq.12, f32[512]{0:T(512)S(1)} %copy-done.6, f32[512]{0:T(512)S(1)} %copy-done.7), kind=kOutput, calls=%fused_computation.15 | convolution fusion | flops 2427584512 | bytes 16519169 | tf_op jit(solution)/shard_map/dot_general | solution.py:54
  98.4 0.0 copy-start.3
  98.4 0.0 copy-start.4
  98.4 0.0 reduce-scatter.3.cloned.1.call-update
  98.4 0.0 copy-start.2
  98.4 0.0 all-gather.2.cloned.1.call-start
  98.5 76.5 %reduce-scatter.3.cloned.1.call-done = f32[16,4608]{1,0:T(8,128)} async-done(((f32[256,4608]{1,0:T(8,128)}), f32[16,4608]{1,0:T(8,128)}) %reduce-scatter.3.cloned.1.call-update) | async-done | bytes 294928 | tf_op jit(solution)/shard_map/reduce_scatter | solution.py:53
  175.0 0.0 copy-done.3
  175.0 1.1 multiply_reduce_fusion.1
  176.1 0.0 copy-done.4
  176.1 1.7 multiply_convert_fusion.1
  177.8 0.0 all-gather.2.cloned.1.call-update
  177.9 0.0 reduce-scatter.5.cloned.1.call-start
  177.9 41.6 %all-gather.2.cloned.1.call-done = bf16[256,4608]{1,0:T(8,128)(2,1)} async-done(((bf16[16,4608]{1,0:T(8,128)(2,1)}), bf16[256,4608]{1,0:T(8,128)(2,1)}) %all-gather.2.cloned.1.call-update) | async-done | bytes 2359312 | tf_op jit(solution)/shard_map/all_gather | solution.py:62
  219.5 2.9 fusion.35
  222.4 0.0 copy-done
  222.5 0.0 copy-done.2
  222.5 6.6 %fusion.9 = f32[256,4608]{1,0:T(8,128)} fusion(bf16[144,4608]{1,0:T(8,128)(2,1)S(1)} %copy-done, bf16[256,4608]{1,0:T(8,128)(2,1)} %all-gather.2.cloned.1.call-done, bf16[4608,144]{0,1:T(8,128)(2,1)S(1)} %copy-done.2, f32[256,144]{0,1:T(8,128)S(1)} %fusion.35), kind=kOutput, calls=%fused_computation.12 | convolution fusion | flops 679845888 | bytes 9879552 | tf_op jit(solution)/shard_map/dot_general | solution.py:65
  229.1 0.0 copy-start.1
  229.1 0.0 copy-start.5
  229.1 0.0 reduce-scatter.5.cloned.1.call-update
  229.1 74.4 %reduce-scatter.5.cloned.1.call-done = f32[16,4608]{1,0:T(8,128)} async-done(((f32[256,4608]{1,0:T(8,128)}), f32[16,4608]{1,0:T(8,128)}) %reduce-scatter.5.cloned.1.call-update) | async-done | bytes 294928 | tf_op jit(solution)/shard_map/reduce_scatter | solution.py:64
  303.5 1.1 multiply_reduce_fusion
  304.7 0.0 copy-done.1
  304.7 0.0 copy-done.5
  304.7 1.7 add_convert_fusion
  (2 shorter events, 0.0 us)
Async XLA Ops:
  6.5 215.9 %copy-start = (bf16[144,4608]{1,0:T(8,128)(2,1)S(1)}, bf16[144,4608]{1,0:T(8,128)(2,1)}, u32[]{:S(2)}) copy-start(bf16[144,4608]{1,0:T(8,128)(2,1)} %param.20) | copy-start | bytes 3981316
  6.5 82.5 %copy-start.6 = (f32[512]{0:T(512)S(1)}, f32[512]{0:T(512)}, u32[]{:S(2)}) copy-start(f32[512]{0:T(512)} %param.14) | copy-start | bytes 6148
  6.5 82.5 %copy-start.7 = (f32[512]{0:T(512)S(1)}, f32[512]{0:T(512)}, u32[]{:S(2)}) copy-start(f32[512]{0:T(512)} %param.13) | copy-start | bytes 6148
  6.5 168.4 %reduce-scatter.3.cloned.1.call-start = ((), (), s32[]{:S(2)}) async-start(), calls=%async_computation.2 | async-start | bytes 5013504 | tf_op jit(solution)/shard_map/reduce_scatter | solution.py:53
  6.5 1.8 collective-permute-start
  9.4 10.2 %collective-permute-start.1 = (bf16[32,4608]{1,0:T(8,128)(2,1)S(1)}, bf16[32,4608]{1,0:T(8,128)(2,1)S(1)}, u32[]{:S(2)}, u32[]{:S(2)}) collective-permute-start(bf16[32,4608]{1,0:T(8,128)(2,1)S(1)} %maximum_select_fusion.10), channel_id=1, source_target_pairs={{0,2},{1,3},{2,0},{3,1},{4,6},{5,7},{6,4},{7,5},{8,10},{9,11},{10,... | collective-permute-start | bytes 884744 | tf_op jit(solution)/shard_map/ppermute | solution.py:14
  19.7 15.0 %collective-permute-start.2 = (bf16[64,4608]{1,0:T(8,128)(2,1)S(1)}, bf16[64,4608]{1,0:T(8,128)(2,1)}, u32[]{:S(2)}, u32[]{:S(2)}) collective-permute-start(bf16[64,4608]{1,0:T(8,128)(2,1)S(1)} %maximum_select_fusion.5), channel_id=1, source_target_pairs={{0,4},{1,5},{2,6},{3,7},{4,0},{5,1},{6,2},{7,3},{8,12},{9,13},{10,... | collective-permute-start | bytes 1769480 | tf_op jit(solution)/shard_map/ppermute | solution.py:14
  36.1 52.9 %collective-permute-start.3 = (bf16[128,4608]{1,0:T(8,128)(2,1)S(1)}, bf16[128,4608]{1,0:T(8,128)(2,1)}, u32[]{:S(2)}, u32[]{:S(2)}) collective-permute-start(bf16[128,4608]{1,0:T(8,128)(2,1)S(1)} %maximum_select_fusion.4), channel_id=1, source_target_pairs={{0,8},{1,9},{2,10},{3,11},{4,12},{5,13},{6,14},{7,15},{8,0},{9,1},... | collective-permute-start | bytes 3538952 | tf_op jit(solution)/shard_map/ppermute | solution.py:14
  98.4 76.6 %copy-start.3 = (f32[4608]{0:T(1024)S(1)}, f32[4608]{0:T(1024)}, u32[]{:S(2)}) copy-start(f32[4608]{0:T(1024)} %param.16) | copy-start | bytes 55300
  98.4 77.7 %copy-start.4 = (f32[4608]{0:T(1024)S(1)}, f32[4608]{0:T(1024)}, u32[]{:S(2)}) copy-start(f32[4608]{0:T(1024)} %param.17) | copy-start | bytes 55300
  98.4 124.0 %copy-start.2 = (bf16[4608,144]{0,1:T(8,128)(2,1)S(1)}, bf16[4608,144]{0,1:T(8,128)(2,1)}, u32[]{:S(2)}) copy-start(bf16[4608,144]{0,1:T(8,128)(2,1)} %param.19) | copy-start | bytes 3981316
  98.4 121.1 %all-gather.2.cloned.1.call-start = ((), (), s32[]{:S(2)}) async-start(), calls=%async_computation.3 | async-start | bytes 2506752 | tf_op jit(solution)/shard_map/all_gather | solution.py:62
  177.9 125.7 %reduce-scatter.5.cloned.1.call-start = ((), (), s32[]{:S(2)}) async-start(), calls=%async_computation.4 | async-start | bytes 5013504 | tf_op jit(solution)/shard_map/reduce_scatter | solution.py:64
  229.1 75.6 %copy-start.1 = (f32[16,4608]{1,0:T(8,128)S(1)}, f32[16,4608]{1,0:T(8,128)}, u32[]{:S(2)}) copy-start(f32[16,4608]{1,0:T(8,128)} %reduce-scatter.3.cloned.1.call-done) | copy-start | bytes 884740
  229.1 75.6 %copy-start.5 = (f32[4608]{0:T(1024)S(1)}, f32[4608]{0:T(1024)}, u32[]{:S(2)}) copy-start(f32[4608]{0:T(1024)} %param.21) | copy-start | bytes 55300
Sparse Core Ops, SparseCore 0:
  98.5 76.4 reduce-scatter.2
  178.0 41.4 all-gather.1
  229.2 74.2 reduce-scatter.4
